TPU v7x, 32 devices: a whole 2x2x4 slice. The times are simulated.
32 devices in a mesh: parts: 2 (over x), row: 8 (over z, core), col: 2 (over y).
Axes of the slice: x: 2, y: 2, z: 4, core: 2. Of those that a mesh axis runs over, the one named last changes fastest.
Arguments:
- pair_features_map: bfloat16 [64, 1024, 512], P(None, ('parts', 'row'), 'col'), parts along dimension 1, may hold values from -6 to 6
- labels: int32 [1024, 512], P(('parts', 'row', 'col')), parts along dimension 0, may hold values from 0 to 36, as said below
- lengths: int32 [2], P('parts'), parts along dimension 0, may hold values from 256 to 512
- conv_weight: bfloat16 [3, 3, 64, 64], replicated, may hold values from -0.25 to 0.25
- conv_bias: float32 [64], replicated, may hold values from -3 to 3
- head_weight: bfloat16 [37, 64], replicated, may hold values from -2.390625 to 2.390625
- head_bias: float32 [37], replicated, may hold values from -4 to 4
Outputs:
- pair_gradient: bfloat16 [64, 1024, 512], P(None, ('parts', 'row'), 'col'), parts along dimension 1
- grad_conv_weight: float32 [6, 3, 64, 64], P('parts'), parts along dimension 0
- grad_conv_bias: float32 [128], P('parts'), parts along dimension 0
- grad_head_weight: float32 [74, 64], P('parts'), parts along dimension 0
- grad_head_bias: float32 [74], P('parts'), parts along dimension 0
- loss: float32 [2], P('parts'), parts along dimension 0
There are 2 independent parts, one for each index of `parts`. A program takes and returns all parts, laid end to end along the dimension named above; an argument that names none is the same for every part. Nothing has to cross between parts.
Inputs may be any that keep to these rules, and one draw needn't show every extreme that they name: labels[i, j] equals labels[j, i] for every pair.
All inputs are finite; a program needn't handle non-finite values.
Results may differ from a plain program's by a relative error of at most 0.0067.
Values may be sent and summed in bfloat16 or wider, within the bound.
No kernel may reach another device: no remote copies, remote signals or barrier semaphores. Data moves between devices by JAX's collectives and lax.ppermute only.
A program may use at most 128 MiB of HBM per device.

v0:
```python
import jax
import jax.numpy as jnp
from jax import lax
from jax.sharding import PartitionSpec as P

DILATION_STEP = 4


def with_halo(cells, sides, width):
    for axis, dim in sides:
        count = lax.axis_size(axis)
        ends = count - 1
        head = lax.slice_in_dim(cells, 0, width, axis=dim)
        tail = lax.slice_in_dim(cells, cells.shape[dim] - width, cells.shape[dim], axis=dim)
        cells = jnp.concatenate(
            [
                lax.ppermute(tail, axis, [(i, (i + 1) % count) for i in range(ends)]),
                cells,
                lax.ppermute(head, axis, [((i + 1) % count, i) for i in range(ends)]),
            ],
            axis=dim,
        )
    return cells


def tile_to_band(field):
    channels, patch_rows, patch_columns = field.shape
    width = lax.axis_size("col")
    split = field.reshape(channels, width, patch_rows // width, patch_columns)
    moved = lax.all_to_all(split, "col", split_axis=1, concat_axis=3, tiled=True)
    return moved.reshape(channels, patch_rows // width, width * patch_columns)


def band_to_tile(field):
    channels, band_rows, length_cols = field.shape
    width = lax.axis_size("col")
    split = field.reshape(channels, band_rows, width, length_cols // width)
    moved = lax.all_to_all(split, "col", split_axis=2, concat_axis=1, tiled=True)
    return moved.reshape(channels, width * band_rows, length_cols // width)


def reorder_back(moved, channels, band_rows, length_cols):
    return jnp.transpose(moved, (0, 3, 2, 1)).reshape(channels, band_rows, length_cols)


def mirror_features(field):
    channels, band_rows, length_cols = field.shape
    bands = lax.axis_size(("row", "col"))
    blocks = field.reshape(channels, band_rows, bands, band_rows)
    moved = lax.all_to_all(blocks, ("row", "col"), split_axis=2, concat_axis=2, tiled=True)
    return reorder_back(moved, channels, band_rows, length_cols)


def per_device(pair_features_map, labels, lengths, conv_weight, conv_bias, head_weight, head_bias):
    channels, patch_rows, patch_columns = pair_features_map.shape
    nbins = head_weight.shape[0]
    bordered_input = with_halo(pair_features_map, (("row", 1), ("col", 2)), DILATION_STEP)
    before_activation = (
        jnp.zeros((channels, patch_rows, patch_columns), jnp.float32) + conv_bias[:, None, None]
    )
    for offset_row in range(3):
        for offset_column in range(3):
            sliding_patch = bordered_input[
                :,
                DILATION_STEP * offset_row : DILATION_STEP * offset_row + patch_rows,
                DILATION_STEP * offset_column : DILATION_STEP * offset_column + patch_columns,
            ]
            before_activation = before_activation + jnp.einsum(
                "oc,cij->oij",
                conv_weight[offset_row, offset_column],
                sliding_patch,
                preferred_element_type=jnp.float32,
            )
    hidden_tile = jnp.where(
        before_activation > 0, before_activation, jnp.expm1(jnp.minimum(before_activation, 0.0))
    ).astype(jnp.bfloat16)
    hidden = tile_to_band(hidden_tile)
    band_rows, length_cols = (hidden.shape[1], hidden.shape[2])
    hidden_mirror = mirror_features(hidden)
    direct = jnp.einsum("kc,cij->kij", head_weight, hidden, preferred_element_type=jnp.float32)
    opposite = jnp.einsum(
        "kc,cij->kij", head_weight, hidden_mirror, preferred_element_type=jnp.float32
    )
    logits = 0.5 * (direct + opposite) + head_bias[:, None, None]
    band = lax.axis_index(("row", "col"))
    row_ids = band * band_rows + lax.broadcasted_iota(jnp.int32, (band_rows, length_cols), 0)
    col_ids = lax.broadcasted_iota(jnp.int32, (band_rows, length_cols), 1)
    extent = lengths[0]
    valid = ((row_ids < extent) & (col_ids < extent)).astype(jnp.float32)
    count = (extent * extent).astype(jnp.float32)
    onehot = (lax.broadcasted_iota(jnp.int32, (nbins, 1, 1), 0) == labels[None]).astype(jnp.float32)
    lse = jnp.log(jnp.sum(jnp.exp(logits), axis=0))
    picked = jnp.sum(onehot * logits, axis=0)
    loss_local = jnp.sum(valid * (lse - picked))
    dlogits = (valid[None] * (jnp.exp(logits - lse[None]) - onehot) / count).astype(jnp.bfloat16)
    head_grad = jnp.einsum("kij,cij->kc", dlogits, hidden, preferred_element_type=jnp.float32)
    head_bias_grad = jnp.sum(dlogits.astype(jnp.float32), axis=(1, 2))
    tile_grad = band_to_tile(dlogits)
    back = jnp.einsum("kc,kij->cij", head_weight, tile_grad, preferred_element_type=jnp.float32)
    slope = jnp.where(before_activation > 0, 1.0, jnp.exp(jnp.minimum(before_activation, 0.0)))
    preact_gradient = (back * slope).astype(jnp.bfloat16)
    preact_gradient_bordered = with_halo(preact_gradient, (("row", 1), ("col", 2)), DILATION_STEP)
    grad_field = jnp.zeros((channels, patch_rows, patch_columns), jnp.float32)
    tap_rows = []
    for offset_row in range(3):
        tap_cols = []
        for offset_column in range(3):
            sliding_patch = bordered_input[
                :,
                DILATION_STEP * offset_row : DILATION_STEP * offset_row + patch_rows,
                DILATION_STEP * offset_column : DILATION_STEP * offset_column + patch_columns,
            ]
            tap_cols.append(
                jnp.einsum(
                    "oij,cij->oc",
                    preact_gradient,
                    sliding_patch,
                    preferred_element_type=jnp.float32,
                )
            )
            row_begin = DILATION_STEP * (2 - offset_row)
            column_begin = DILATION_STEP * (2 - offset_column)
            source = preact_gradient_bordered[
                :, row_begin : row_begin + patch_rows, column_begin : column_begin + patch_columns
            ]
            grad_field = grad_field + jnp.einsum(
                "oc,oij->cij",
                conv_weight[offset_row, offset_column],
                source,
                preferred_element_type=jnp.float32,
            )
        tap_rows.append(jnp.stack(tap_cols))
    conv_grad = jnp.stack(tap_rows)
    conv_bias_grad = jnp.sum(preact_gradient.astype(jnp.float32), axis=(1, 2))
    conv_grad, conv_bias_grad, head_grad, head_bias_grad, loss_total = lax.psum(
        (conv_grad, conv_bias_grad, head_grad, head_bias_grad, loss_local), ("row", "col")
    )
    loss = (loss_total / count).reshape(1)
    return (
        grad_field.astype(jnp.bfloat16),
        conv_grad,
        conv_bias_grad,
        head_grad,
        head_bias_grad,
        loss,
    )


def solution(mesh):
    return jax.shard_map(
        per_device,
        mesh=mesh,
        in_specs=(
            P(None, ("parts", "row"), "col"),
            P(("parts", "row", "col"), None),
            P("parts"),
            P(),
            P(),
            P(),
            P(),
        ),
        out_specs=(
            P(None, ("parts", "row"), "col"),
            P("parts", None, None, None),
            P("parts"),
            P("parts", None),
            P("parts"),
            P("parts"),
        ),
        check_vma=False,
    )
```

profile of v0, /device:TPU:0, one launch (start us, length us, event | category | flops | bytes accessed | tf_op | source)
XLA Modules:
  0.0 410.8 jit_solution(8611053157606536604)
XLA Ops:
  13.8 4.4 %fusion.60 = f32[64,64,256]{2,0,1:T(8,128)} fusion(bf16[3,3,64,64]{3,2,1,0:T(8,128)(2,1)} %param.10, bf16[64,64,256]{2,1,0:T(8,128)(2,1)S(1)} %copy-done.10), kind=kOutput, calls=%fused_computation.100 | convolution fusion | flops 134217728 | bytes 6307840 | tf_op jit(solution)/shard_map/oc,cij->oij/dot_general | solution.py:68
  25.1 4.9 %collective-permute-start.2 = (bf16[64,72,4]{1,0,2:T(8,128)(2,1)}, bf16[64,72,4]{1,0,2:T(8,128)(2,1)}, u32[]{:S(2)}, u32[]{:S(2)}) collective-permute-start(bf16[64,72,4]{1,0,2:T(8,128)(2,1)} %copy.58), channel_id=1, source_target_pairs={{0,1},{2,3},{4,5},{6,7},{8,9},{10,11},{12,13},{14,15},{16,17},{18,... | collective-permute-start | bytes 110600 | tf_op jit(solution)/shard_map/ppermute | solution.py:17
  33.7 4.3 %fusion.41 = f32[64,256,64]{1,2,0:T(8,128)} fusion(bf16[64,64,256]{2,0,1:T(8,128)(2,1)} %copy-done.7, bf16[64,4,256]{2,0,1:T(8,128)(2,1)} %copy-done.23, bf16[3,3,64,64]{3,2,1,0:T(8,128)(2,1)} %param.10), kind=kOutput, calls=%fused_computation.67 | convolution fusion | flops 138412032 | bytes 6438912 | tf_op jit(solution)/shard_map/oc,cij->oij/dot_general | solution.py:68
  58.1 3.9 fusion.56
  65.9 13.3 %fusion = (bf16[64,64,256]{2,0,1:T(8,128)(2,1)S(1)}, f32[64,64,256]{2,0,1:T(8,128)}) fusion(bf16[64,72,4]{2,0,1:T(8,128)(2,1)S(1)} %copy.62, bf16[64,72,256]{2,0,1:T(8,128)(2,1)S(1)} %constant_dynamic-update-slice_fusion, bf16[3,3,64,64]{3,2,1,0:T(8,128)(2,1)} %param.10, f32[64,256,64]{1,2,0:T(8,128)} %fusion.43, f32[64,256,64]{1,2,0:T(8,128)} %fusion.47, ...), kind=kOutput, calls=%fused_computation.6 | convolution fusion | flops 152043520 | bytes 42258688 | tf_op jit(solution)/shard_map/oc,cij->oij/dot_general | solution.py:68
  80.4 29.7 %all_to_all.35 = bf16[64,2,32,256]{3,2,0,1:T(8,128)(2,1)} all-to-all(bf16[64,2,32,256]{3,2,0,1:T(8,128)(2,1)S(1)} %copy.65), channel_id=1, replica_groups=mesh['parts'=2,'row'=8,'col'=2] {'col'}, dimensions={1} | all-to-all | bytes 4194304 | tf_op jit(solution)/shard_map/all_to_all | solution.py:30
  110.1 5.0 %copy.66 = bf16[64,2,32,256]{0,3,1,2:T(8,128)(2,1)} copy(bf16[64,2,32,256]{3,2,0,1:T(8,128)(2,1)} %all_to_all.35) | data formatting | bytes 4194304 | tf_op jit(solution)/shard_map/all_to_all | solution.py:30
  115.0 5.3 %copy.126 = bf16[64,32,16,32]{0,3,1,2:T(8,128)(2,1)} copy(bf16[64,32,16,32]{0,3,2,1:T(8,128)(2,1)} %bitcast.202) | data formatting | bytes 4194304 | tf_op jit(solution)/shard_map/reshape;reshape | solution.py:49
  120.3 7.5 %reshape.99 = bf16[16,2,32768]{2,1,0:T(2,128)(2,1)} reshape(bf16[16,32,32,64]{3,2,1,0:T(8,128)(2,1)} %bitcast.205) | data formatting | bytes 4194304
  127.9 6.9 %all-to-all-start.1 = ((bf16[16,2,32768]{2,1,0:T(2,128)(2,1)}), bf16[16,2,32768]{2,1,0:T(2,128)(2,1)}, u32[]{:S(2)}, u32[]{:S(2)}) async-start(bf16[16,2,32768]{2,1,0:T(2,128)(2,1)} %reshape.99), calls=%async_computation.1 | async-start | bytes 4194304 | tf_op jit(solution)/shard_map/all_to_all | solution.py:50
  136.7 6.1 %fusion.93 = f32[32,512,37]{1,2,0:T(8,128)} fusion(bf16[64,32,512]{0,2,1:T(8,128)(2,1)} %bitcast.203, bf16[37,64]{1,0:T(8,128)(2,1)S(1)} %copy-done), kind=kOutput, calls=%fused_computation.133 | convolution fusion | flops 77594624 | bytes 4526720 | tf_op jit(solution)/shard_map/kc,cij->kij/dot_general | solution.py:80
  142.9 34.0 %all-to-all-done.1 = bf16[16,2,32768]{2,1,0:T(2,128)(2,1)} async-done(((bf16[16,2,32768]{2,1,0:T(2,128)(2,1)}), bf16[16,2,32768]{2,1,0:T(2,128)(2,1)}, u32[]{:S(2)}, u32[]{:S(2)}) %all-to-all-start.1) | async-done | bytes 2097184 | tf_op jit(solution)/shard_map/all_to_all | solution.py:50
  176.9 7.4 %reshape.100 = bf16[16,32,32,64]{3,2,1,0:T(8,128)(2,1)} reshape(bf16[16,2,32768]{2,1,0:T(2,128)(2,1)} %all-to-all-done.1) | data formatting | bytes 4194304
  184.3 7.9 %fusion.10 = (f32[32,512]{1,0:T(8,128)S(1)}, f32[32,512]{1,0:T(8,128)S(1)}, f32[32,512,37]{1,2,0:T(8,128)S(1)}) fusion(s32[32,512]{1,0:T(8,128)} %param.8, f32[37]{0:T(128)} %param.13, f32[32,512,37]{1,2,0:T(8,128)} %fusion.93, bf16[37,64]{1,0:T(8,128)(2,1)S(1)} %copy-done, bf16[64,32,512]{0,1,2:T(8,128)(2,1)} %bitcast.207), kind=kOutput, calls=%fused_computation.32 | convolution fusion | flops 81805312 | bytes 7148308 | tf_op jit(solution)/shard_map/kc,cij->kij/dot_general | solution.py:81
  201.5 4.5 %all-to-all-start.2 = ((bf16[37,32,2,256]{3,1,0,2:T(8,128)(2,1)}), bf16[37,32,2,256]{3,1,0,2:T(8,128)(2,1)}, u32[]{:S(2)}, u32[]{:S(2)}) async-start(bf16[37,32,2,256]{3,1,0,2:T(8,128)(2,1)} %copy.72), calls=%async_computation.2 | async-start | bytes 2424832 | tf_op jit(solution)/shard_map/all_to_all | solution.py:38
  206.2 4.1 convolution_bitcast_fusion.7
  210.3 10.8 %all-to-all-done.2 = bf16[37,32,2,256]{3,1,0,2:T(8,128)(2,1)} async-done(((bf16[37,32,2,256]{3,1,0,2:T(8,128)(2,1)}), bf16[37,32,2,256]{3,1,0,2:T(8,128)(2,1)}, u32[]{:S(2)}, u32[]{:S(2)}) %all-to-all-start.2) | async-done | bytes 1212448 | tf_op jit(solution)/shard_map/all_to_all | solution.py:38
  223.1 4.2 %convert_reduce_fusion = (f32[64]{0:T(128)}, bf16[64,64,256]{2,0,1:T(8,128)(2,1)S(1)}) fusion(f32[64,64,256]{2,0,1:T(8,128)} %get-tuple-element.45, bf16[37,64,256]{2,0,1:T(8,128)(2,1)S(1)} %bitcast.208, bf16[37,64]{1,0:T(8,128)(2,1)S(1)} %copy-done), kind=kOutput, calls=%fused_computation.17 | convolution fusion | flops 84934592 | bytes 7508864 | tf_op jit(solution)/shard_map/kc,kij->cij/dot_general | solution.py:99
  243.0 4.4 %collective-permute-start.4 = (bf16[64,4,256]{2,0,1:T(8,128)(2,1)S(1)}, bf16[64,4,256]{2,0,1:T(8,128)(2,1)S(1)}, u32[]{:S(2)}, u32[]{:S(2)}) collective-permute-start(bf16[64,4,256]{2,0,1:T(8,128)(2,1)S(1)} %get-tuple-element.39), channel_id=1, source_target_pairs={{0,2},{2,4},{4,6},{6,8},{8,10},{10,12},{12,14},{1,3},{3,5},{5,7},{... | collective-permute-start | bytes 393224 | tf_op jit(solution)/shard_map/ppermute | solution.py:17
  249.0 62.7 %all-reduce = (f32[64]{0:T(128)}, f32[37,64]{1,0:T(8,128)}, f32[37]{0:T(128)}, f32[]{:T(128)}) all-reduce(f32[64]{0:T(128)S(1)} %copy-done.30, f32[37,64]{1,0:T(8,128)S(1)} %copy-done.26, f32[37]{0:T(128)S(1)} %get-tuple-element.30, f32[]{:T(128)} %get-tuple-element.42), channel_id=1, replica_groups=mesh['parts'=2,'row'=8,'col'=2] {'row','col'}, use_global_device_ids=true, to_apply=%region_3.4 | all-reduce | flops 2470 | bytes 19760 | tf_op jit(solution)/shard_map/psum | solution.py:135
  324.1 5.9 %collective-permute-start.7 = (bf16[64,72,4]{1,0,2:T(8,128)(2,1)}, bf16[64,72,4]{1,0,2:T(8,128)(2,1)}, u32[]{:S(2)}, u32[]{:S(2)}) collective-permute-start(bf16[64,72,4]{1,0,2:T(8,128)(2,1)} %copy.78), channel_id=1, source_target_pairs={{0,1},{2,3},{4,5},{6,7},{8,9},{10,11},{12,13},{14,15},{16,17},{18,... | collective-permute-start | bytes 110600 | tf_op jit(solution)/shard_map/ppermute | solution.py:17
  343.5 6.5 %maximum_maximum_fusion = (bf16[64,72,260]{2,0,1:T(8,128)(2,1)S(1)}, bf16[64,72,260]{2,0,1:T(8,128)(2,1)S(1)}) fusion(bf16[64,4,256]{2,0,1:T(8,128)(2,1)S(1)} %copy-done.16, bf16[64,64,256]{2,0,1:T(8,128)(2,1)S(1)} %copy-done.3, bf16[64,4,256]{2,0,1:T(8,128)(2,1)S(1)} %copy-done.18, bf16[64,72,4]{2,0,1:T(8,128)(2,1)} %copy.79, bf16[64,72,4]{2,0,1:T(8,128)(2,1)S(1)} %copy.75), kind=kLoop, calls=%fused_computation.23 | loop fusion | flops 19169280 | bytes 7225344 | tf_op jit(solution)/shard_map/concatenate | solution.py:15
  364.3 10.8 %fusion.24 = bf16[64,64,256]{2,0,1:T(8,128)(2,1)S(1)} fusion(f32[64,256,64]{1,2,0:T(8,128)} %fusion.16, f32[64,256,64]{1,2,0:T(8,128)} %fusion.29, f32[64,256,64]{1,2,0:T(8,128)} %fusion.31, f32[64,256,64]{1,2,0:T(8,128)S(1)} %copy-done.12, f32[64,256,64]{1,2,0:T(8,128)} %fusion.33, f32[64,256,64]{1,2,0:T(8,128)} %fusion.35, f32[64,256,64]{1,2,0:T(8,128)} %fusion.37, ...), kind=kOutput, calls=%fused_computation.50 | convolution fusion | flops 143654912 | bytes 37765120 | tf_op jit(solution)/shard_map/oc,oij->cij/dot_general | solution.py:126
  377.5 23.2 %all-reduce.3.cloned.1.call-done = f32[3,3,64,64]{3,2,1,0:T(8,128)} async-done(((f32[3,3,64,64]{3,2,1,0:T(8,128)}), f32[3,3,64,64]{3,2,1,0:T(8,128)}) %all-reduce.3.cloned.1.call-update) | async-done | bytes 147472 | tf_op jit(solution)/shard_map/psum | solution.py:135
  (132 shorter events, 115.8 us)
Async XLA Ops:
  7.2 129.6 %copy-start = (bf16[37,64]{1,0:T(8,128)(2,1)S(1)}, bf16[37,64]{1,0:T(8,128)(2,1)}, u32[]{:S(2)}) copy-start(bf16[37,64]{1,0:T(8,128)(2,1)} %param.12) | copy-start | bytes 14212
  7.2 6.6 %copy-start.10 = (bf16[64,64,256]{2,1,0:T(8,128)(2,1)S(1)}, bf16[64,64,256]{2,1,0:T(8,128)(2,1)}, u32[]{:S(2)}) copy-start(bf16[64,64,256]{2,1,0:T(8,128)(2,1)} %param.7) | copy-start | bytes 6291460
  10.1 8.1 %copy-start.7 = (bf16[64,64,256]{2,0,1:T(8,128)(2,1)}, bf16[64,64,256]{2,0,1:T(8,128)(2,1)S(1)}, u32[]{:S(2)}) copy-start(bf16[64,64,256]{2,0,1:T(8,128)(2,1)S(1)} %copy.55) | copy-start | bytes 6291460
  10.2 8.1 %collective-permute-start = (bf16[64,4,256]{2,0,1:T(8,128)(2,1)S(1)}, bf16[64,4,256]{2,0,1:T(8,128)(2,1)S(1)}, u32[]{:S(2)}, u32[]{:S(2)}) collective-permute-start(bf16[64,4,256]{2,0,1:T(8,128)(2,1)S(1)} %get-tuple-element.40), channel_id=1, source_target_pairs={{0,2},{2,4},{4,6},{6,8},{8,10},{10,12},{12,14},{1,3},{3,5},{5,7},{... | collective-permute-start | bytes 393224 | tf_op jit(solution)/shard_map/ppermute | solution.py:17
  12.5 6.9 %collective-permute-start.1 = (bf16[64,4,256]{2,0,1:T(8,128)(2,1)S(1)}, bf16[64,4,256]{2,0,1:T(8,128)(2,1)S(1)}, u32[]{:S(2)}, u32[]{:S(2)}) collective-permute-start(bf16[64,4,256]{2,0,1:T(8,128)(2,1)S(1)} %get-tuple-element.41), channel_id=1, source_target_pairs={{2,0},{4,2},{6,4},{8,6},{10,8},{12,10},{14,12},{3,1},{5,3},{7,5},{... | collective-permute-start | bytes 393224 | tf_op jit(solution)/shard_map/ppermute | solution.py:19
  25.1 16.2 %collective-permute-start.2 = (bf16[64,72,4]{1,0,2:T(8,128)(2,1)}, bf16[64,72,4]{1,0,2:T(8,128)(2,1)}, u32[]{:S(2)}, u32[]{:S(2)}) collective-permute-start(bf16[64,72,4]{1,0,2:T(8,128)(2,1)} %copy.58), channel_id=1, source_target_pairs={{0,1},{2,3},{4,5},{6,7},{8,9},{10,11},{12,13},{14,15},{16,17},{18,... | collective-permute-start | bytes 110600 | tf_op jit(solution)/shard_map/ppermute | solution.py:17
  32.0 19.4 %collective-permute-start.3 = (bf16[64,72,4]{1,0,2:T(8,128)(2,1)}, bf16[64,72,4]{1,0,2:T(8,128)(2,1)}, u32[]{:S(2)}, u32[]{:S(2)}) collective-permute-start(bf16[64,72,4]{1,0,2:T(8,128)(2,1)} %copy.61), channel_id=1, source_target_pairs={{1,0},{3,2},{5,4},{7,6},{9,8},{11,10},{13,12},{15,14},{17,16},{19,... | collective-permute-start | bytes 110600 | tf_op jit(solution)/shard_map/ppermute | solution.py:19
  127.9 49.0 %all-to-all-start.1 = ((bf16[16,2,32768]{2,1,0:T(2,128)(2,1)}), bf16[16,2,32768]{2,1,0:T(2,128)(2,1)}, u32[]{:S(2)}, u32[]{:S(2)}) async-start(bf16[16,2,32768]{2,1,0:T(2,128)(2,1)} %reshape.99), calls=%async_computation.1 | async-start | bytes 4194304 | tf_op jit(solution)/shard_map/all_to_all | solution.py:50
  184.3 7.9 %copy-start.29 = (pred[32]{0:T(512)(128)(4,1)S(1)}, pred[32]{0:T(512)(128)(4,1)}, u32[]{:S(2)}) copy-start(pred[32]{0:T(512)(128)(4,1)} %copy-done.28) | copy-start | bytes 100
  184.3 8.6 %copy-start.25 = (f32[32,512]{1,0:T(8,128)S(1)}, f32[32,512]{1,0:T(8,128)}, u32[]{:S(2)}) copy-start(f32[32,512]{1,0:T(8,128)} %and_convert_fusion) | copy-start | bytes 196612
  184.3 8.6 %copy-start.27 = (s32[32,512]{1,0:T(8,128)S(1)}, s32[32,512]{1,0:T(8,128)}, u32[]{:S(2)}) copy-start(s32[32,512]{1,0:T(8,128)} %param.8) | copy-start | bytes 196612
  201.5 19.6 %all-to-all-start.2 = ((bf16[37,32,2,256]{3,1,0,2:T(8,128)(2,1)}), bf16[37,32,2,256]{3,1,0,2:T(8,128)(2,1)}, u32[]{:S(2)}, u32[]{:S(2)}) async-start(bf16[37,32,2,256]{3,1,0,2:T(8,128)(2,1)} %copy.72), calls=%async_computation.2 | async-start | bytes 2424832 | tf_op jit(solution)/shard_map/all_to_all | solution.py:38
  206.0 194.7 %all-reduce.3.cloned.1.call-start = ((), (), s32[]{:S(2)}) async-start(), calls=%async_computation.3 | async-start | bytes 589824 | tf_op jit(solution)/shard_map/psum | solution.py:135
  227.3 20.9 %copy-start.2 = (bf16[64,64,256]{2,0,1:T(8,128)(2,1)}, bf16[64,64,256]{2,0,1:T(8,128)(2,1)S(1)}, u32[]{:S(2)}) copy-start(bf16[64,64,256]{2,0,1:T(8,128)(2,1)S(1)} %get-tuple-element.48) | copy-start | bytes 6291460
  238.1 9.4 %copy-start.9 = (bf16[64,64,256]{2,0,1:T(8,128)(2,1)S(1)}, bf16[64,64,256]{2,0,1:T(8,128)(2,1)}, u32[]{:S(2)}) copy-start(bf16[64,64,256]{2,0,1:T(8,128)(2,1)} %copy-done.7) | copy-start | bytes 6291460
  238.1 9.4 %copy-start.24 = (bf16[64,4,256]{2,0,1:T(8,128)(2,1)S(1)}, bf16[64,4,256]{2,0,1:T(8,128)(2,1)}, u32[]{:S(2)}) copy-start(bf16[64,4,256]{2,0,1:T(8,128)(2,1)} %copy-done.23) | copy-start | bytes 393220
  241.7 71.4 %collective-permute-start.5 = (bf16[64,4,256]{2,0,1:T(8,128)(2,1)S(1)}, bf16[64,4,256]{2,0,1:T(8,128)(2,1)S(1)}, u32[]{:S(2)}, u32[]{:S(2)}) collective-permute-start(bf16[64,4,256]{2,0,1:T(8,128)(2,1)S(1)} %get-tuple-element.38), channel_id=1, source_target_pairs={{2,0},{4,2},{6,4},{8,6},{10,8},{12,10},{14,12},{3,1},{5,3},{7,5},{... | collective-permute-start | bytes 393224 | tf_op jit(solution)/shard_map/ppermute | solution.py:19
  243.0 70.1 %collective-permute-start.4 = (bf16[64,4,256]{2,0,1:T(8,128)(2,1)S(1)}, bf16[64,4,256]{2,0,1:T(8,128)(2,1)S(1)}, u32[]{:S(2)}, u32[]{:S(2)}) collective-permute-start(bf16[64,4,256]{2,0,1:T(8,128)(2,1)S(1)} %get-tuple-element.39), channel_id=1, source_target_pairs={{0,2},{2,4},{4,6},{6,8},{8,10},{10,12},{12,14},{1,3},{3,5},{5,7},{... | collective-permute-start | bytes 393224 | tf_op jit(solution)/shard_map/ppermute | solution.py:17
  318.0 12.0 %copy-start.3 = (bf16[64,64,256]{2,0,1:T(8,128)(2,1)S(1)}, bf16[64,64,256]{2,0,1:T(8,128)(2,1)}, u32[]{:S(2)}) copy-start(bf16[64,64,256]{2,0,1:T(8,128)(2,1)} %copy-done.2) | copy-start | bytes 6291460
  318.0 12.0 %copy-start.15 = (bf16[64,4,256]{2,0,1:T(8,128)(2,1)S(1)}, bf16[64,4,256]{2,0,1:T(8,128)(2,1)}, u32[]{:S(2)}) copy-start(bf16[64,4,256]{2,0,1:T(8,128)(2,1)} %copy-done.14) | copy-start | bytes 393220
  320.8 16.2 %collective-permute-start.6 = (bf16[64,72,4]{1,0,2:T(8,128)(2,1)S(1)}, bf16[64,72,4]{1,0,2:T(8,128)(2,1)}, u32[]{:S(2)}, u32[]{:S(2)}) collective-permute-start(bf16[64,72,4]{1,0,2:T(8,128)(2,1)S(1)} %copy.74), channel_id=1, source_target_pairs={{1,0},{3,2},{5,4},{7,6},{9,8},{11,10},{13,12},{15,14},{17,16},{19,... | collective-permute-start | bytes 110600 | tf_op jit(solution)/shard_map/ppermute | solution.py:19
  324.1 9.4 %copy-start.18 = (bf16[64,4,256]{2,0,1:T(8,128)(2,1)S(1)}, bf16[64,4,256]{2,0,1:T(8,128)(2,1)}, u32[]{:S(2)}) copy-start(bf16[64,4,256]{2,0,1:T(8,128)(2,1)} %copy-done.17) | copy-start | bytes 393220
  324.1 15.7 %collective-permute-start.7 = (bf16[64,72,4]{1,0,2:T(8,128)(2,1)}, bf16[64,72,4]{1,0,2:T(8,128)(2,1)}, u32[]{:S(2)}, u32[]{:S(2)}) collective-permute-start(bf16[64,72,4]{1,0,2:T(8,128)(2,1)} %copy.78), channel_id=1, source_target_pairs={{0,1},{2,3},{4,5},{6,7},{8,9},{10,11},{12,13},{14,15},{16,17},{18,... | collective-permute-start | bytes 110600 | tf_op jit(solution)/shard_map/ppermute | solution.py:17
  364.3 38.2 %copy-start.1 = (bf16[37,64]{1,0:T(8,128)(2,1)S(1)}, bf16[37,64]{1,0:T(8,128)(2,1)}, u32[]{:S(2)}) copy-start(bf16[37,64]{1,0:T(8,128)(2,1)} %param.12) | copy-start | bytes 14212
  (19 other events, 57.2 us)
Sparse Core Ops, SparseCore 0:
  313.2 87.4 all-reduce.2
where the time goes:
time: 418 us; the launch traced here: 411 us
  matrix products  113 us (27%)
  blocking collectives  92.3 us (22%)
  local copies, waits for them, and re-layouts  72.9 us (17%)
  waiting for transfers between devices  68.1 us (16%)
  starting transfers between devices  34.7 us (8%)
  between operations  17.4 us (4%)
  other arithmetic  12.7 us (3%)
    psum x1, blocking collectives, per_device(): lax.psum((conv_grad, conv_bias_grad, head_grad, head_bias_grad, loss_loca...  62.7 us
    dot_general x9, matrix products, per_device(): jnp.einsum('oc,cij->oij', conv_weight[offset_row, offset_column], sliding...  44.2 us
    dot_general x9, matrix products, per_device(): jnp.einsum('oc,oij->cij', conv_weight[offset_row, offset_column], source,...  35.5 us
    all_to_all x1, waiting for transfers between devices, mirror_features(): lax.all_to_all(blocks, ('row', 'col'), split_axis=2, concat_axis=2, tiled...  34 us
    all_to_all x1, blocking collectives, tile_to_band(): lax.all_to_all(split, 'col', split_axis=1, concat_axis=3, tiled=True)  29.7 us
    unnamed x71, local copies, waits for them, and re-layouts  27.2 us
    psum x1, waiting for transfers between devices, per_device(): lax.psum((conv_grad, conv_bias_grad, head_grad, head_bias_grad, loss_loca...  23.2 us
    ppermute x4, starting transfers between devices, with_halo(): lax.ppermute(tail, axis, [(i, (i + 1) % count) for i in range(ends)])  17.6 us
  transfers between devices with their start and end apart: 11, of which 3 were waited for; matrix products, arithmetic and copies ran while one was open for 23% of the time, Pallas kernels for 0%

commit v1 on v0

--- a/solution.py
+++ b/solution.py
@@ -132,8 +132,9 @@
         tap_rows.append(jnp.stack(tap_cols))
     conv_grad = jnp.stack(tap_rows)
     conv_bias_grad = jnp.sum(preact_gradient.astype(jnp.float32), axis=(1, 2))
-    conv_grad, conv_bias_grad, head_grad, head_bias_grad, loss_total = lax.psum(
-        (conv_grad, conv_bias_grad, head_grad, head_bias_grad, loss_local), ("row", "col")
+    forms_store = lambda arr: lax.psum(lax.psum(arr, axis_name="col"), axis_name="row")
+    conv_grad, conv_bias_grad, head_grad, head_bias_grad, loss_total = forms_store(
+        (conv_grad, conv_bias_grad, head_grad, head_bias_grad, loss_local)
     )
     loss = (loss_total / count).reshape(1)
     return (

time: 418 us -> 386 us (0.923)
  the two profiles are of different devices: /device:TPU:0 before, /device:TPU:1 now
where the time goes in v1:
time: 386 us; the launch traced here: 379 us
  matrix products  113 us (29%)
  local copies, waits for them, and re-layouts  72.2 us (19%)
  waiting for transfers between devices  65.8 us (17%)
  blocking collectives  58.7 us (15%)
  starting transfers between devices  39 us (10%)
  between operations  17.4 us (5%)
  other arithmetic  12.7 us (3%)
    dot_general x9, matrix products, per_device(): jnp.einsum('oc,cij->oij', conv_weight[offset_row, offset_column], sliding...  44.2 us
    all_to_all x1, waiting for transfers between devices, mirror_features(): lax.all_to_all(blocks, ('row', 'col'), split_axis=2, concat_axis=2, tiled...  36.1 us
    dot_general x9, matrix products, per_device(): jnp.einsum('oc,oij->cij', conv_weight[offset_row, offset_column], source,...  35.5 us
    all_to_all x1, blocking collectives, tile_to_band(): lax.all_to_all(split, 'col', split_axis=1, concat_axis=3, tiled=True)  28.5 us
    unnamed x61, local copies, waits for them, and re-layouts  26 us
    psum x1, blocking collectives, per_device(): lax.psum(lax.psum(arr, axis_name='col'), axis_name='row')  24 us
    ppermute x4, starting transfers between devices, with_halo(): lax.ppermute(tail, axis, [(i, (i + 1) % count) for i in range(ends)])  21.1 us
    psum x1, waiting for transfers between devices, per_device(): lax.psum(lax.psum(arr, axis_name='col'), axis_name='row')  15.7 us
  transfers between devices with their start and end apart: 12, of which 4 were waited for; matrix products, arithmetic and copies ran while one was open for 25% of the time, Pallas kernels for 0%

profile of v1, /device:TPU:1, one launch (start us, length us, event | category | flops | bytes accessed | tf_op | source)
XLA Modules:
  0.0 378.6 jit_solution(1891917622029278764)
XLA Ops:
  10.2 4.6 %collective-permute-start = (bf16[64,4,256]{2,0,1:T(8,128)(2,1)S(1)}, bf16[64,4,256]{2,0,1:T(8,128)(2,1)S(1)}, u32[]{:S(2)}, u32[]{:S(2)}) collective-permute-start(bf16[64,4,256]{2,0,1:T(8,128)(2,1)S(1)} %get-tuple-element.44), channel_id=1, source_target_pairs={{0,2},{2,4},{4,6},{6,8},{8,10},{10,12},{12,14},{1,3},{3,5},{5,7},{... | collective-permute-start | bytes 393224 | tf_op jit(solution)/shard_map/ppermute | solution.py:17
  16.7 4.4 %fusion.60 = f32[64,64,256]{2,0,1:T(8,128)} fusion(bf16[3,3,64,64]{3,2,1,0:T(8,128)(2,1)} %param.10, bf16[64,64,256]{2,1,0:T(8,128)(2,1)S(1)} %copy-done.10), kind=kOutput, calls=%fused_computation.100 | convolution fusion | flops 134217728 | bytes 6307840 | tf_op jit(solution)/shard_map/oc,cij->oij/dot_general | solution.py:68
  35.3 4.3 %fusion.41 = f32[64,256,64]{1,2,0:T(8,128)} fusion(bf16[64,64,256]{2,0,1:T(8,128)(2,1)} %copy-done.7, bf16[64,4,256]{2,0,1:T(8,128)(2,1)} %copy-done.18, bf16[3,3,64,64]{3,2,1,0:T(8,128)(2,1)} %param.10), kind=kOutput, calls=%fused_computation.67 | convolution fusion | flops 138412032 | bytes 6438912 | tf_op jit(solution)/shard_map/oc,cij->oij/dot_general | solution.py:68
  67.6 13.3 %fusion = (bf16[64,64,256]{2,0,1:T(8,128)(2,1)S(1)}, f32[64,64,256]{2,0,1:T(8,128)}) fusion(bf16[64,72,4]{2,0,1:T(8,128)(2,1)S(1)} %copy.62, bf16[64,72,256]{2,0,1:T(8,128)(2,1)S(1)} %constant_dynamic-update-slice_fusion, bf16[3,3,64,64]{3,2,1,0:T(8,128)(2,1)} %param.10, f32[64,256,64]{1,2,0:T(8,128)} %fusion.43, f32[64,256,64]{1,2,0:T(8,128)} %fusion.47, ...), kind=kOutput, calls=%fused_computation.6 | convolution fusion | flops 152043520 | bytes 42258688 | tf_op jit(solution)/shard_map/oc,cij->oij/dot_general | solution.py:68
  82.1 28.5 %all_to_all.35 = bf16[64,2,32,256]{3,2,0,1:T(8,128)(2,1)} all-to-all(bf16[64,2,32,256]{3,2,0,1:T(8,128)(2,1)S(1)} %copy.65), channel_id=1, replica_groups=mesh['parts'=2,'row'=8,'col'=2] {'col'}, dimensions={1} | all-to-all | bytes 4194304 | tf_op jit(solution)/shard_map/all_to_all | solution.py:30
  110.6 5.0 %copy.66 = bf16[64,2,32,256]{0,3,1,2:T(8,128)(2,1)} copy(bf16[64,2,32,256]{3,2,0,1:T(8,128)(2,1)} %all_to_all.35) | data formatting | bytes 4194304 | tf_op jit(solution)/shard_map/all_to_all | solution.py:30
  115.6 5.3 %copy.126 = bf16[64,32,16,32]{0,3,1,2:T(8,128)(2,1)} copy(bf16[64,32,16,32]{0,3,2,1:T(8,128)(2,1)} %bitcast.202) | data formatting | bytes 4194304 | tf_op jit(solution)/shard_map/reshape;reshape | solution.py:49
  120.9 7.6 %reshape.99 = bf16[16,2,32768]{2,1,0:T(2,128)(2,1)} reshape(bf16[16,32,32,64]{3,2,1,0:T(8,128)(2,1)} %bitcast.205) | data formatting | bytes 4194304
  128.4 6.4 %all-to-all-start.1 = ((bf16[16,2,32768]{2,1,0:T(2,128)(2,1)}), bf16[16,2,32768]{2,1,0:T(2,128)(2,1)}, u32[]{:S(2)}, u32[]{:S(2)}) async-start(bf16[16,2,32768]{2,1,0:T(2,128)(2,1)} %reshape.99), calls=%async_computation.1 | async-start | bytes 4194304 | tf_op jit(solution)/shard_map/all_to_all | solution.py:50
  136.7 6.1 %fusion.93 = f32[32,512,37]{1,2,0:T(8,128)} fusion(bf16[64,32,512]{0,2,1:T(8,128)(2,1)} %bitcast.203, bf16[37,64]{1,0:T(8,128)(2,1)S(1)} %copy-done), kind=kOutput, calls=%fused_computation.133 | convolution fusion | flops 77594624 | bytes 4526720 | tf_op jit(solution)/shard_map/kc,cij->kij/dot_general | solution.py:80
  142.9 36.1 %all-to-all-done.1 = bf16[16,2,32768]{2,1,0:T(2,128)(2,1)} async-done(((bf16[16,2,32768]{2,1,0:T(2,128)(2,1)}), bf16[16,2,32768]{2,1,0:T(2,128)(2,1)}, u32[]{:S(2)}, u32[]{:S(2)}) %all-to-all-start.1) | async-done | bytes 2097184 | tf_op jit(solution)/shard_map/all_to_all | solution.py:50
  179.0 7.5 %reshape.100 = bf16[16,32,32,64]{3,2,1,0:T(8,128)(2,1)} reshape(bf16[16,2,32768]{2,1,0:T(2,128)(2,1)} %all-to-all-done.1) | data formatting | bytes 4194304
  186.5 7.9 %fusion.10 = (f32[32,512]{1,0:T(8,128)S(1)}, f32[32,512]{1,0:T(8,128)S(1)}, f32[32,512,37]{1,2,0:T(8,128)S(1)}) fusion(s32[32,512]{1,0:T(8,128)} %param.8, f32[37]{0:T(128)} %param.13, f32[32,512,37]{1,2,0:T(8,128)} %fusion.93, bf16[37,64]{1,0:T(8,128)(2,1)S(1)} %copy-done, bf16[64,32,512]{0,1,2:T(8,128)(2,1)} %bitcast.207), kind=kOutput, calls=%fused_computation.32 | convolution fusion | flops 81805312 | bytes 7148308 | tf_op jit(solution)/shard_map/kc,cij->kij/dot_general | solution.py:81
  203.7 4.5 %all-to-all-start.2 = ((bf16[37,32,2,256]{3,1,0,2:T(8,128)(2,1)}), bf16[37,32,2,256]{3,1,0,2:T(8,128)(2,1)}, u32[]{:S(2)}, u32[]{:S(2)}) async-start(bf16[37,32,2,256]{3,1,0,2:T(8,128)(2,1)} %copy.72), calls=%async_computation.2 | async-start | bytes 2424832 | tf_op jit(solution)/shard_map/all_to_all | solution.py:38
  212.4 9.8 %all-to-all-done.2 = bf16[37,32,2,256]{3,1,0,2:T(8,128)(2,1)} async-done(((bf16[37,32,2,256]{3,1,0,2:T(8,128)(2,1)}), bf16[37,32,2,256]{3,1,0,2:T(8,128)(2,1)}, u32[]{:S(2)}, u32[]{:S(2)}) %all-to-all-start.2) | async-done | bytes 1212448 | tf_op jit(solution)/shard_map/all_to_all | solution.py:38
  224.2 4.2 %convert_reduce_fusion = (f32[64]{0:T(128)}, bf16[64,64,256]{2,0,1:T(8,128)(2,1)S(1)}) fusion(f32[64,64,256]{2,0,1:T(8,128)} %get-tuple-element.49, bf16[37,64,256]{2,0,1:T(8,128)(2,1)S(1)} %bitcast.208, bf16[37,64]{1,0:T(8,128)(2,1)S(1)} %copy-done), kind=kOutput, calls=%fused_computation.17 | convolution fusion | flops 84934592 | bytes 7508864 | tf_op jit(solution)/shard_map/kc,kij->cij/dot_general | solution.py:99
  244.7 7.5 %collective-permute-start.4 = (bf16[64,4,256]{2,0,1:T(8,128)(2,1)S(1)}, bf16[64,4,256]{2,0,1:T(8,128)(2,1)S(1)}, u32[]{:S(2)}, u32[]{:S(2)}) collective-permute-start(bf16[64,4,256]{2,0,1:T(8,128)(2,1)S(1)} %get-tuple-element.43), channel_id=1, source_target_pairs={{0,2},{2,4},{4,6},{6,8},{8,10},{10,12},{12,14},{1,3},{3,5},{5,7},{... | collective-permute-start | bytes 393224 | tf_op jit(solution)/shard_map/ppermute | solution.py:17
  253.8 6.2 %all-reduce.1 = (f32[64]{0:T(128)S(1)}, f32[37,64]{1,0:T(8,128)S(1)}, f32[37]{0:T(128)S(1)}, f32[]{:T(128)}) all-reduce(f32[64]{0:T(128)S(1)} %copy-done.25, f32[37,64]{1,0:T(8,128)S(1)} %copy-done.21, f32[37]{0:T(128)S(1)} %get-tuple-element.34, f32[]{:T(128)} %get-tuple-element.46), channel_id=1, replica_groups=mesh['parts'=2,'row'=8,'col'=2] {'col'}, use_global_device_ids=true, to_apply=%region_4.5 | all-reduce | flops 2470 | bytes 19760 | tf_op jit(solution)/shard_map/psum | solution.py:135
  259.9 24.0 %all-reduce = (f32[64]{0:T(128)}, f32[37,64]{1,0:T(8,128)}, f32[37]{0:T(128)}, f32[]{:T(128)}) all-reduce(f32[64]{0:T(128)S(1)} %get-tuple-element.30, f32[37,64]{1,0:T(8,128)S(1)} %get-tuple-element.31, f32[37]{0:T(128)S(1)} %get-tuple-element.32, f32[]{:T(128)} %get-tuple-element.33), channel_id=1, replica_groups=mesh['parts'=2,'row'=8,'col'=2] {'row'}, use_global_device_ids=true, to_apply=%region_5.6 | all-reduce | flops 2470 | bytes 19760 | tf_op jit(solution)/shard_map/psum | solution.py:135
  295.7 5.2 %collective-permute-start.7 = (bf16[64,72,4]{1,0,2:T(8,128)(2,1)}, bf16[64,72,4]{1,0,2:T(8,128)(2,1)}, u32[]{:S(2)}, u32[]{:S(2)}) collective-permute-start(bf16[64,72,4]{1,0,2:T(8,128)(2,1)} %copy.78), channel_id=1, source_target_pairs={{0,1},{2,3},{4,5},{6,7},{8,9},{10,11},{12,13},{14,15},{16,17},{18,... | collective-permute-start | bytes 110600 | tf_op jit(solution)/shard_map/ppermute | solution.py:17
  307.9 4.1 %all-reduce.5.cloned.1.call-done = f32[3,3,64,64]{3,2,1,0:T(8,128)} async-done(((f32[3,3,64,64]{3,2,1,0:T(8,128)}), f32[3,3,64,64]{3,2,1,0:T(8,128)}) %all-reduce.5.cloned.1.call-update) | async-done | bytes 147472 | tf_op jit(solution)/shard_map/psum | solution.py:135
  318.6 6.5 %maximum_maximum_fusion = (bf16[64,72,260]{2,0,1:T(8,128)(2,1)S(1)}, bf16[64,72,260]{2,0,1:T(8,128)(2,1)S(1)}) fusion(bf16[64,4,256]{2,0,1:T(8,128)(2,1)S(1)} %collective-permute-done.5, bf16[64,64,256]{2,0,1:T(8,128)(2,1)S(1)} %copy-done.3, bf16[64,4,256]{2,0,1:T(8,128)(2,1)S(1)} %collective-permute-done.4, bf16[64,72,4]{2,0,1:T(8,128)(2,1)} %copy.79, ...), kind=kLoop, calls=%fused_computation.23 | loop fusion | flops 19169280 | bytes 7225344 | tf_op jit(solution)/shard_map/concatenate | solution.py:15
  339.4 10.8 %fusion.24 = bf16[64,64,256]{2,0,1:T(8,128)(2,1)S(1)} fusion(f32[64,256,64]{1,2,0:T(8,128)} %fusion.16, f32[64,256,64]{1,2,0:T(8,128)} %fusion.29, f32[64,256,64]{1,2,0:T(8,128)} %fusion.31, f32[64,256,64]{1,2,0:T(8,128)S(1)} %copy-done.12, f32[64,256,64]{1,2,0:T(8,128)} %fusion.33, f32[64,256,64]{1,2,0:T(8,128)} %fusion.35, f32[64,256,64]{1,2,0:T(8,128)} %fusion.37, ...), kind=kOutput, calls=%fused_computation.50 | convolution fusion | flops 143654912 | bytes 37765120 | tf_op jit(solution)/shard_map/oc,oij->cij/dot_general | solution.py:126
  352.8 15.7 %all-reduce.7.cloned.1.call-done = f32[3,3,64,64]{3,2,1,0:T(8,128)} async-done(((f32[3,3,64,64]{3,2,1,0:T(8,128)}), f32[3,3,64,64]{3,2,1,0:T(8,128)}) %all-reduce.7.cloned.1.call-update) | async-done | bytes 147472 | tf_op jit(solution)/shard_map/psum | solution.py:135
  (126 shorter events, 125.8 us)
Async XLA Ops:
  7.2 129.6 %copy-start = (bf16[37,64]{1,0:T(8,128)(2,1)S(1)}, bf16[37,64]{1,0:T(8,128)(2,1)}, u32[]{:S(2)}) copy-start(bf16[37,64]{1,0:T(8,128)(2,1)} %param.12) | copy-start | bytes 14212
  7.2 9.5 %copy-start.10 = (bf16[64,64,256]{2,1,0:T(8,128)(2,1)S(1)}, bf16[64,64,256]{2,1,0:T(8,128)(2,1)}, u32[]{:S(2)}) copy-start(bf16[64,64,256]{2,1,0:T(8,128)(2,1)} %param.7) | copy-start | bytes 6291460
  10.1 11.0 %copy-start.7 = (bf16[64,64,256]{2,0,1:T(8,128)(2,1)}, bf16[64,64,256]{2,0,1:T(8,128)(2,1)S(1)}, u32[]{:S(2)}) copy-start(bf16[64,64,256]{2,0,1:T(8,128)(2,1)S(1)} %copy.55) | copy-start | bytes 6291460
  10.2 10.9 %collective-permute-start = (bf16[64,4,256]{2,0,1:T(8,128)(2,1)S(1)}, bf16[64,4,256]{2,0,1:T(8,128)(2,1)S(1)}, u32[]{:S(2)}, u32[]{:S(2)}) collective-permute-start(bf16[64,4,256]{2,0,1:T(8,128)(2,1)S(1)} %get-tuple-element.44), channel_id=1, source_target_pairs={{0,2},{2,4},{4,6},{6,8},{8,10},{10,12},{12,14},{1,3},{3,5},{5,7},{... | collective-permute-start | bytes 393224 | tf_op jit(solution)/shard_map/ppermute | solution.py:17
  14.8 8.2 %collective-permute-start.1 = (bf16[64,4,256]{2,0,1:T(8,128)(2,1)S(1)}, bf16[64,4,256]{2,0,1:T(8,128)(2,1)S(1)}, u32[]{:S(2)}, u32[]{:S(2)}) collective-permute-start(bf16[64,4,256]{2,0,1:T(8,128)(2,1)S(1)} %get-tuple-element.45), channel_id=1, source_target_pairs={{2,0},{4,2},{6,4},{8,6},{10,8},{12,10},{14,12},{3,1},{5,3},{7,5},{... | collective-permute-start | bytes 393224 | tf_op jit(solution)/shard_map/ppermute | solution.py:19
  27.9 15.1 %collective-permute-start.2 = (bf16[64,72,4]{1,0,2:T(8,128)(2,1)}, bf16[64,72,4]{1,0,2:T(8,128)(2,1)}, u32[]{:S(2)}, u32[]{:S(2)}) collective-permute-start(bf16[64,72,4]{1,0,2:T(8,128)(2,1)} %copy.58), channel_id=1, source_target_pairs={{0,1},{2,3},{4,5},{6,7},{8,9},{10,11},{12,13},{14,15},{16,17},{18,... | collective-permute-start | bytes 110600 | tf_op jit(solution)/shard_map/ppermute | solution.py:17
  33.7 19.4 %collective-permute-start.3 = (bf16[64,72,4]{1,0,2:T(8,128)(2,1)}, bf16[64,72,4]{1,0,2:T(8,128)(2,1)}, u32[]{:S(2)}, u32[]{:S(2)}) collective-permute-start(bf16[64,72,4]{1,0,2:T(8,128)(2,1)} %copy.61), channel_id=1, source_target_pairs={{1,0},{3,2},{5,4},{7,6},{9,8},{11,10},{13,12},{15,14},{17,16},{19,... | collective-permute-start | bytes 110600 | tf_op jit(solution)/shard_map/ppermute | solution.py:19
  128.4 50.6 %all-to-all-start.1 = ((bf16[16,2,32768]{2,1,0:T(2,128)(2,1)}), bf16[16,2,32768]{2,1,0:T(2,128)(2,1)}, u32[]{:S(2)}, u32[]{:S(2)}) async-start(bf16[16,2,32768]{2,1,0:T(2,128)(2,1)} %reshape.99), calls=%async_computation.1 | async-start | bytes 4194304 | tf_op jit(solution)/shard_map/all_to_all | solution.py:50
  186.5 7.9 %copy-start.24 = (pred[32]{0:T(512)(128)(4,1)S(1)}, pred[32]{0:T(512)(128)(4,1)}, u32[]{:S(2)}) copy-start(pred[32]{0:T(512)(128)(4,1)} %copy-done.23) | copy-start | bytes 100
  186.5 8.6 %copy-start.20 = (f32[32,512]{1,0:T(8,128)S(1)}, f32[32,512]{1,0:T(8,128)}, u32[]{:S(2)}) copy-start(f32[32,512]{1,0:T(8,128)} %and_convert_fusion) | copy-start | bytes 196612
  186.5 8.6 %copy-start.22 = (s32[32,512]{1,0:T(8,128)S(1)}, s32[32,512]{1,0:T(8,128)}, u32[]{:S(2)}) copy-start(s32[32,512]{1,0:T(8,128)} %param.8) | copy-start | bytes 196612
  203.7 18.5 %all-to-all-start.2 = ((bf16[37,32,2,256]{3,1,0,2:T(8,128)(2,1)}), bf16[37,32,2,256]{3,1,0,2:T(8,128)(2,1)}, u32[]{:S(2)}, u32[]{:S(2)}) async-start(bf16[37,32,2,256]{3,1,0,2:T(8,128)(2,1)} %copy.72), calls=%async_computation.2 | async-start | bytes 2424832 | tf_op jit(solution)/shard_map/all_to_all | solution.py:38
  208.2 103.9 %all-reduce.5.cloned.1.call-start = ((), (), s32[]{:S(2)}) async-start(), calls=%async_computation.3 | async-start | bytes 589824 | tf_op jit(solution)/shard_map/psum | solution.py:135
  228.4 24.6 %copy-start.2 = (bf16[64,64,256]{2,0,1:T(8,128)(2,1)}, bf16[64,64,256]{2,0,1:T(8,128)(2,1)S(1)}, u32[]{:S(2)}) copy-start(bf16[64,64,256]{2,0,1:T(8,128)(2,1)S(1)} %get-tuple-element.52) | copy-start | bytes 6291460
  239.2 13.1 %copy-start.9 = (bf16[64,64,256]{2,0,1:T(8,128)(2,1)S(1)}, bf16[64,64,256]{2,0,1:T(8,128)(2,1)}, u32[]{:S(2)}) copy-start(bf16[64,64,256]{2,0,1:T(8,128)(2,1)} %copy-done.7) | copy-start | bytes 6291460
  239.2 13.1 %copy-start.19 = (bf16[64,4,256]{2,0,1:T(8,128)(2,1)S(1)}, bf16[64,4,256]{2,0,1:T(8,128)(2,1)}, u32[]{:S(2)}) copy-start(bf16[64,4,256]{2,0,1:T(8,128)(2,1)} %copy-done.18) | copy-start | bytes 393220
  242.8 42.7 %collective-permute-start.5 = (bf16[64,4,256]{2,0,1:T(8,128)(2,1)S(1)}, bf16[64,4,256]{2,0,1:T(8,128)(2,1)S(1)}, u32[]{:S(2)}, u32[]{:S(2)}) collective-permute-start(bf16[64,4,256]{2,0,1:T(8,128)(2,1)S(1)} %get-tuple-element.42), channel_id=1, source_target_pairs={{2,0},{4,2},{6,4},{8,6},{10,8},{12,10},{14,12},{3,1},{5,3},{7,5},{... | collective-permute-start | bytes 393224 | tf_op jit(solution)/shard_map/ppermute | solution.py:19
  244.7 8.3 %copy-start.17 = (bf16[64,4,256]{2,0,1:T(8,128)(2,1)S(1)}, bf16[64,4,256]{2,0,1:T(8,128)(2,1)}, u32[]{:S(2)}) copy-start(bf16[64,4,256]{2,0,1:T(8,128)(2,1)} %copy-done.15) | copy-start | bytes 393220
  244.7 40.7 %collective-permute-start.4 = (bf16[64,4,256]{2,0,1:T(8,128)(2,1)S(1)}, bf16[64,4,256]{2,0,1:T(8,128)(2,1)S(1)}, u32[]{:S(2)}, u32[]{:S(2)}) collective-permute-start(bf16[64,4,256]{2,0,1:T(8,128)(2,1)S(1)} %get-tuple-element.43), channel_id=1, source_target_pairs={{0,2},{2,4},{4,6},{6,8},{8,10},{10,12},{12,14},{1,3},{3,5},{5,7},{... | collective-permute-start | bytes 393224 | tf_op jit(solution)/shard_map/ppermute | solution.py:17
  285.4 83.0 %all-reduce.7.cloned.1.call-start = ((), (), s32[]{:S(2)}) async-start(), calls=%async_computation.4 | async-start | bytes 589824 | tf_op jit(solution)/shard_map/psum | solution.py:135
  289.0 12.0 %copy-start.3 = (bf16[64,64,256]{2,0,1:T(8,128)(2,1)S(1)}, bf16[64,64,256]{2,0,1:T(8,128)(2,1)}, u32[]{:S(2)}) copy-start(bf16[64,64,256]{2,0,1:T(8,128)(2,1)} %copy-done.2) | copy-start | bytes 6291460
  292.4 19.6 %collective-permute-start.6 = (bf16[64,72,4]{1,0,2:T(8,128)(2,1)}, bf16[64,72,4]{1,0,2:T(8,128)(2,1)}, u32[]{:S(2)}, u32[]{:S(2)}) collective-permute-start(bf16[64,72,4]{1,0,2:T(8,128)(2,1)} %copy.74), channel_id=1, source_target_pairs={{1,0},{3,2},{5,4},{7,6},{9,8},{11,10},{13,12},{15,14},{17,16},{19,... | collective-permute-start | bytes 110600 | tf_op jit(solution)/shard_map/ppermute | solution.py:19
  295.7 19.2 %collective-permute-start.7 = (bf16[64,72,4]{1,0,2:T(8,128)(2,1)}, bf16[64,72,4]{1,0,2:T(8,128)(2,1)}, u32[]{:S(2)}, u32[]{:S(2)}) collective-permute-start(bf16[64,72,4]{1,0,2:T(8,128)(2,1)} %copy.78), channel_id=1, source_target_pairs={{0,1},{2,3},{4,5},{6,7},{8,9},{10,11},{12,13},{14,15},{16,17},{18,... | collective-permute-start | bytes 110600 | tf_op jit(solution)/shard_map/ppermute | solution.py:17
  339.4 30.7 %copy-start.1 = (bf16[37,64]{1,0:T(8,128)(2,1)S(1)}, bf16[37,64]{1,0:T(8,128)(2,1)}, u32[]{:S(2)}) copy-start(bf16[37,64]{1,0:T(8,128)(2,1)} %param.12) | copy-start | bytes 14212
  (15 other events, 44.6 us)
Sparse Core Ops, SparseCore 0:
  285.5 26.4 all-reduce.4
  314.3 54.0 all-reduce.6
